TPU v7x, 512 devices: a whole 4x4x16 slice. The times are simulated.
512 devices in a mesh: prow: 32 (over z, core), pcol: 16 (over x, y).
Axes of the slice: x: 4, y: 4, z: 16, core: 2. Of those that a mesh axis runs over, the one named last changes fastest.
Arguments:
- trailing: bfloat16 [8, 8192, 2, 4096], P(None, 'prow', None, 'pcol'), may hold values from -6 to 6
- panel: bfloat16 [256, 8, 8192], P('pcol', None, 'prow'), may hold values from -1 to 1
- lower_inverse: bfloat16 [256, 256], replicated
- upper_inverse: bfloat16 [256, 256], replicated
- pivots: int32 [256], replicated, may hold values from 0 to 65535, as said below
Outputs:
- updated: bfloat16 [8, 8192, 2, 4096], P(None, 'prow', None, 'pcol')
Inputs may be any that keep to these rules, and one draw needn't show every extreme that they name: `pivots`: the entries are distinct; entry i is either i or a row index of 256 or more. Entry 0 is 0 and entry 1 is 65535.
All inputs are finite; a program needn't handle non-finite values.
Results may differ from a plain program's by a relative error of at most 0.0054.
Values may be sent and summed in bfloat16 or wider, within the bound.
A program may use at most 64 MiB of HBM per device.

v0:
```python
import jax
import jax.numpy as jnp
from jax import lax
from jax.sharding import PartitionSpec as P


def from_root(x, axis, root):
    mine = lax.axis_index(axis) == root
    return lax.psum(jnp.where(mine, x, jnp.zeros_like(x)), axis)


def contract_lead(left_side, right_side):
    return lax.dot_general(
        left_side, right_side, (((0,), (0,)), ((), ())), preferred_element_type=jnp.float32
    )


def per_device(trailing, panel, lower_inverse, upper_inverse, pivots):
    row_blocks, block_size, col_blocks, col_size = trailing.shape
    local_rows = row_blocks * block_size
    matrix = trailing.reshape(local_rows, col_blocks * col_size)
    panel_rows = panel.reshape(panel.shape[0], local_rows)
    prow_count = lax.axis_size("prow")
    prow_index = lax.axis_index("prow")
    head_rows = jnp.arange(block_size, dtype=jnp.int32)
    pivot_owner = pivots // block_size % prow_count
    pivot_local = pivots // (block_size * prow_count) * block_size + pivots % block_size
    pivot_here = pivot_owner == prow_index
    fetched = jnp.take(matrix, jnp.where(pivot_here, pivot_local, 0), axis=0)
    picked = jnp.where(pivot_here[:, None], fetched, jnp.zeros_like(fetched))
    old_top = matrix[:block_size]
    at_root = prow_index == 0
    source = picked[None]
    gathered_top = lax.psum(source, "prow").astype(jnp.float32).astype(jnp.bfloat16)
    solved = jnp.dot(lower_inverse, gathered_top[0], preferred_element_type=jnp.float32).astype(
        jnp.bfloat16
    )
    root_top = from_root(old_top, "prow", 0)
    local_index = jnp.arange(local_rows, dtype=jnp.int32)
    global_rows = (
        local_index // block_size * prow_count + prow_index
    ) * block_size + local_index % block_size
    matches = (global_rows[:, None] == pivots[None, :]) & (pivots != head_rows)[None, :]
    incoming = jnp.sum(jnp.where(matches, head_rows[None, :], 0), axis=1)
    has_incoming = jnp.any(matches, axis=1)
    swapped = jnp.where(has_incoming[:, None], jnp.take(root_top, incoming, axis=0), matrix)
    lower_t = contract_lead(upper_inverse, lax.all_gather(panel_rows, "pcol", axis=0, tiled=True))
    lower_t = lower_t.astype(jnp.bfloat16)
    product = contract_lead(lower_t, solved)
    updated = (swapped.astype(jnp.float32) - product).astype(jnp.bfloat16)
    top_block = jnp.where(at_root, solved, updated[:block_size])
    updated = lax.dynamic_update_slice_in_dim(updated, top_block, 0, 0)
    return updated.reshape(trailing.shape)


def solution(mesh):
    placed = (P(None, "prow", None, "pcol"), P("pcol", None, "prow"), P(), P(), P())
    return jax.shard_map(
        per_device,
        mesh=mesh,
        in_specs=placed,
        out_specs=P(None, "prow", None, "pcol"),
        check_vma=False,
    )
```

profile of v0, /device:TPU:1, one launch (start us, length us, event | category | flops | bytes accessed | tf_op | source)
XLA Modules:
  0.0 261.1 jit_solution(12199682226288083791)
XLA Ops:
  7.4 0.0 copy-start
  7.4 0.0 all-reduce.3.cloned.1.call-start
  7.4 0.7 compare_and_fusion.2
  8.1 1.2 broadcast_select_fusion
  9.3 0.7 copy.23
  10.0 2.0 copy.24
  12.1 0.0 copy-start.4
  12.1 1.2 gather_fusion.1
  13.2 0.8 fusion.3
  14.1 0.0 all-reduce.3.cloned.1.call-update
  14.1 0.0 all-gather.2.cloned.1.call-start
  14.1 0.0 copy-done.4
  14.2 0.6 copy.25
  14.8 0.0 all-gather.2.cloned.1.call-update
  14.8 0.0 copy-start.5
  14.8 2.4 copy.22
  17.2 0.0 copy-done.5
  17.2 0.8 fusion
  18.0 0.9 select_reduce_fusion
  18.9 212.9 %all-reduce.3.cloned.1.call-done = (bf16[256,512]{1,0:T(8,128)(2,1)}, bf16[256,512]{1,0:T(8,128)(2,1)}) async-done(((bf16[256,512]{1,0:T(8,128)(2,1)}, bf16[256,512]{1,0:T(8,128)(2,1)}), (bf16[256,512]{1,0:T(8,128)(2,1)}, bf16[256,512]{1,0:T(8,128)(2,1)})) %all-reduce.3.cloned.1.call-update) | async-done | bytes 524304 | tf_op jit(solution)/shard_map/psum | solution.py:34
  231.8 8.6 %gather_fusion = bf16[2048,512]{1,0:T(8,128)(2,1)S(1)} fusion(bf16[256,512]{1,0:T(8,128)(2,1)} %get-tuple-element.6, s32[2048]{0:T(1024)S(1)} %broadcast_clamp_fusion), kind=kCustom, calls=%fused_computation | custom fusion | bytes 4202496 | tf_op jit(solution)/shard_map/jit(_take)/gather | solution.py:46
  240.4 0.0 copy-start.2
  240.4 0.0 copy-start.3
  240.4 2.5 copy.16
  242.8 0.3 convolution_convert_fusion.1
  243.1 0.0 all-gather.2.cloned.1.call-done
  243.2 3.8 %subtract_convert_fusion = bf16[2048,512]{0,1:T(8,128)(2,1)S(1)} fusion(bf16[512,256]{1,0:T(8,128)(2,1)S(1)} %convolution_convert_fusion.1, bf16[2048,512]{0,1:T(8,128)(2,1)} %copy.22, bf16[2048,512]{0,1:T(8,128)(2,1)} %copy.16, pred[2048]{0:T(1024)(128)(4,1)S(1)} %compare_and_fusion.1, pred[2048]{0:T(1024)(128)(4,1)S(1)} %fusion, ...), kind=kOutput, calls=%fused_computation.2 | convolution fusion | flops 811073536 | bytes 7737344 | tf_op jit(solution)/shard_map/dot_general | solution.py:13
  246.9 0.1 fusion.1
  247.1 0.0 copy-start.1
  247.1 1.3 copy-done.1
  248.4 2.3 copy.26
  250.7 3.0 %copy.20 = bf16[8,256,2,256]{3,2,1,0:T(2,128)(2,1)} copy(bf16[8,256,2,256]{1,0,3,2:T(8,128)(2,1)S(1)} %bitcast.32) | data formatting | bytes 4194304 | tf_op jit(solution)/shard_map/reshape | solution.py:53
  (8 shorter events, 0.0 us)
Async XLA Ops:
  7.4 235.8 %copy-start = (bf16[256,256]{1,0:T(8,128)(2,1)S(1)}, bf16[256,256]{1,0:T(8,128)(2,1)}, u32[]{:S(2)}) copy-start(bf16[256,256]{1,0:T(8,128)(2,1)} %param.8) | copy-start | bytes 393220
  7.4 224.4 %all-reduce.3.cloned.1.call-start = ((), (), s32[]{:S(2)}) async-start(), calls=%async_computation.1 | async-start | bytes 1048576 | tf_op jit(solution)/shard_map/psum | solution.py:34
  12.1 2.1 copy-start.4
  14.1 229.0 %all-gather.2.cloned.1.call-start = ((), (), s32[]{:S(2)}) async-start(), calls=%async_computation | async-start | bytes 1114112 | tf_op jit(solution)/shard_map/all_gather | solution.py:47
  14.8 2.4 copy-start.5
  240.4 2.5 copy-start.2
  240.4 2.5 copy-start.3
  247.1 1.3 copy-start.1
Sparse Core Ops, SparseCore 0:
  14.2 217.5 all-reduce.2
Sparse Core Ops, SparseCore 1:
  17.6 61.1 all-gather.1
where the time goes:
time: 261 us
  waiting for transfers between devices  213 us (82%)
  local copies, waits for them, and re-layouts  24.5 us (9%)
  between operations  15 us (6%)
  other arithmetic  4.52 us (2%)
  matrix products  4.05 us (2%)
    psum x1, waiting for transfers between devices, per_device(): lax.psum(source, 'prow').astype(jnp.float32).astype(jnp.bfloat16)  213 us
    gather x2, local copies, waits for them, and re-layouts, per_device(): jnp.take(root_top, incoming, axis=0)  11 us
    unnamed x16, local copies, waits for them, and re-layouts  7.01 us
  transfers between devices with their start and end apart: 2, of which 1 were waited for; matrix products, arithmetic and copies ran while one was open for 6% of the time, Pallas kernels for 0%

commit v1 on v0

--- a/solution.py
+++ b/solution.py
@@ -1,7 +1,15 @@
+import functools
 import jax
 import jax.numpy as jnp
 from jax import lax
 from jax.sharding import PartitionSpec as P
+
+
+def shards_fill(message, comm_axis):
+    return jnp.sum(lax.all_gather(message, comm_axis), axis=0)
+
+
+prepare_sections = functools.partial(shards_fill, comm_axis="prow")
 
 
 def from_root(x, axis, root):
@@ -31,7 +39,7 @@
     old_top = matrix[:block_size]
     at_root = prow_index == 0
     source = picked[None]
-    gathered_top = lax.psum(source, "prow").astype(jnp.float32).astype(jnp.bfloat16)
+    gathered_top = prepare_sections(source).astype(jnp.float32).astype(jnp.bfloat16)
     solved = jnp.dot(lower_inverse, gathered_top[0], preferred_element_type=jnp.float32).astype(
         jnp.bfloat16
     )

time: 261 us -> 380 us (1.46)
  waiting for transfers between devices: 213 us -> 328 us
  other arithmetic: 4.52 us -> 9.26 us
    all_gather x0 -> x1, waiting for transfers between devices: none -> 70.1 us  [shards_fill(): return jnp.sum(lax.all_gather(message, comm_axis), axis=0)]
    all_gather x1, waiting for transfers between devices: 0.03 us -> 50.2 us  [per_device(): lax.all_gather(panel_rows, 'pcol', axis=0, tiled=True)]
    psum x1, waiting for transfers between devices: 213 us -> 207 us  [from_root(): return lax.psum(jnp.where(mine, x, jnp.zeros_like(x)), axis)]
    reduce_sum x0 -> x1, other arithmetic: none -> 4.75 us  [shards_fill(): return jnp.sum(lax.all_gather(message, comm_axis), axis=0)]
  transfers between devices with their start and end apart: 2 -> 3, of which waited for: 1 -> 3; matrix products, arithmetic and copies ran while one was open for 6% -> 7% of each run, Pallas kernels for 0% -> 0%
where the time goes in v1:
time: 380 us; the launch traced here: 379 us
  waiting for transfers between devices  328 us (86%)
  local copies, waits for them, and re-layouts  24.6 us (6%)
  between operations  13.2 us (3%)
  other arithmetic  9.26 us (2%)
  matrix products  3.99 us (1%)
    psum x1, waiting for transfers between devices, from_root(): return lax.psum(jnp.where(mine, x, jnp.zeros_like(x)), axis)  207 us
    all_gather x1, waiting for transfers between devices, shards_fill(): return jnp.sum(lax.all_gather(message, comm_axis), axis=0)  70.1 us
    all_gather x1, waiting for transfers between devices, per_device(): lax.all_gather(panel_rows, 'pcol', axis=0, tiled=True)  50.2 us
    gather x2, local copies, waits for them, and re-layouts, per_device(): jnp.take(root_top, incoming, axis=0)  11.1 us
  transfers between devices with their start and end apart: 3, of which 3 were waited for; matrix products, arithmetic and copies ran while one was open for 7% of the time, Pallas kernels for 0%

profile of v1, /device:TPU:1, one launch (start us, length us, event | category | flops | bytes accessed | tf_op | source)
XLA Modules:
  0.0 378.8 jit_solution(18030564050243366710)
XLA Ops:
  6.5 0.0 copy-start
  6.5 0.0 all-reduce.2.cloned.1.call-start
  6.5 1.2 broadcast_select_fusion
  7.7 0.7 copy.28
  8.5 0.0 all-reduce.2.cloned.1.call-update
  8.5 0.0 all-gather.5.cloned.1.call-start
  8.6 0.7 compare_and_fusion.2
  9.3 2.0 copy.29
  11.3 0.0 copy-start.3
  11.3 1.2 gather_fusion.1
  12.5 0.8 fusion.2
  13.3 0.0 all-gather.5.cloned.1.call-update
  13.3 0.0 all-gather.3.cloned.1.call-start
  13.4 0.6 copy.30
  14.0 0.0 all-gather.3.cloned.1.call-update
  14.1 0.0 copy-start.4
  14.1 2.4 copy.27
  16.5 0.7 fusion
  17.2 0.9 select_reduce_fusion
  18.1 207.3 %all-reduce.2.cloned.1.call-done = bf16[256,512]{1,0:T(8,128)(2,1)} async-done(((bf16[256,512]{1,0:T(8,128)(2,1)}), bf16[256,512]{1,0:T(8,128)(2,1)}) %all-reduce.2.cloned.1.call-update) | async-done | bytes 262160 | tf_op jit(solution)/shard_map/psum | solution.py:17
  225.5 8.6 %gather_fusion = bf16[2048,512]{1,0:T(8,128)(2,1)S(1)} fusion(bf16[256,512]{1,0:T(8,128)(2,1)} %all-reduce.2.cloned.1.call-done, s32[2048]{0:T(1024)S(1)} %broadcast_clamp_fusion), kind=kCustom, calls=%fused_computation | custom fusion | bytes 4202496 | tf_op jit(solution)/shard_map/jit(_take)/gather | solution.py:54
  234.0 2.5 copy.21
  236.5 70.1 %all-gather.5.cloned.1.call-done = bf16[32,1,256,512]{3,2,1,0:T(8,128)(2,1)} async-done(((bf16[1,1,256,512]{3,2,1,0:T(8,128)(2,1)}), bf16[32,1,256,512]{3,2,1,0:T(8,128)(2,1)}) %all-gather.5.cloned.1.call-update) | async-done | bytes 8388624 | tf_op jit(solution)/shard_map/all_gather | solution.py:9
  306.6 4.8 %reduce_sum.25 = bf16[256,512]{1,0:T(8,128)(2,1)S(1)} reduce(bf16[32,1,256,512]{3,2,1,0:T(8,128)(2,1)} %all-gather.5.cloned.1.call-done, bf16[]{:T(256)} %constant.106.clone.1), dimensions={0,1}, to_apply=%region_3.4 | reduce | flops 4063232 | bytes 8650754 | tf_op jit(solution)/shard_map/reduce_sum | solution.py:9
  311.4 0.3 convolution_convert_fusion.1
  311.6 50.2 %all-gather.3.cloned.1.call-done = bf16[256,2048]{1,0:T(8,128)(2,1)} async-done(((bf16[16,2048]{1,0:T(8,128)(2,1)}), bf16[256,2048]{1,0:T(8,128)(2,1)}) %all-gather.3.cloned.1.call-update) | async-done | bytes 1048592 | tf_op jit(solution)/shard_map/all_gather | solution.py:55
  361.8 3.7 subtract_convert_fusion
  365.6 0.1 fusion.1
  365.7 0.0 copy-start.1
  365.7 1.3 copy-done.1
  367.0 2.3 copy.31
  369.3 3.0 copy.25
  (10 shorter events, 0.0 us)
Async XLA Ops:
  6.5 355.3 %copy-start = (bf16[256,256]{1,0:T(8,128)(2,1)S(1)}, bf16[256,256]{1,0:T(8,128)(2,1)}, u32[]{:S(2)}) copy-start(bf16[256,256]{1,0:T(8,128)(2,1)} %param.8) | copy-start | bytes 393220
  6.5 218.9 %all-reduce.2.cloned.1.call-start = ((), (), s32[]{:S(2)}) async-start(), calls=%async_computation | async-start | bytes 524288 | tf_op jit(solution)/shard_map/psum | solution.py:17
  8.5 298.1 %all-gather.5.cloned.1.call-start = ((), (), s32[]{:S(2)}) async-start(), calls=%async_computation.2 | async-start | bytes 8650752 | tf_op jit(solution)/shard_map/all_gather | solution.py:9
  11.3 2.1 copy-start.3
  13.3 348.5 %all-gather.3.cloned.1.call-start = ((), (), s32[]{:S(2)}) async-start(), calls=%async_computation.1 | async-start | bytes 1114112 | tf_op jit(solution)/shard_map/all_gather | solution.py:55
  14.1 2.4 copy-start.4
  236.5 74.8 %copy-start.2 = (bf16[256,256]{1,0:T(8,128)(2,1)S(1)}, bf16[256,256]{1,0:T(8,128)(2,1)}, u32[]{:S(2)}) copy-start(bf16[256,256]{1,0:T(8,128)(2,1)} %param.7) | copy-start | bytes 393220
  365.7 1.3 copy-start.1
Sparse Core Ops, SparseCore 0:
  9.6 215.7 all-reduce.1
  227.6 78.9 all-gather.4
  309.6 52.1 all-gather.2
